TPU v7x, 32 devices: a whole 2x2x4 slice. The times are simulated.
32 devices in a mesh: lon: 8 (over z, core), mem: 4 (over y, x).
Axes of the slice: x: 2, y: 2, z: 4, core: 2. Of those that a mesh axis runs over, the one named last changes fastest.
Arguments:
- members: float32 [32, 4, 192, 256], P('mem', None, 'lon'), may hold values from -6 to 6
- courant_lon: float32 [4, 192, 256], P(None, 'lon'), may hold values from -0.55 to 0.55
- courant_lat: float32 [4, 192, 256], P(None, 'lon'), may hold values from -0.4 to 0.4
- vert_modes: float32 [2, 4], replicated, may hold values from -1 to 1
- horiz_modes: float32 [4, 192, 256], P(None, 'lon'), may hold values from -1 to 1
- obs_index: int32 [16384], P('lon'), may hold values from 0 to 24575
- obs_count: int32 [8], P('lon'), may hold values from 1024 to 2048, as said below
- obs_value: float32 [16384], P('lon'), may hold values from -6 to 6
- obs_var: float32 [16384], P('lon'), may hold values from 2 to 48
Outputs:
- prior_trajectories: float32 [32, 4, 192, 256], P('mem', None, 'lon')
- analysis_mean: float32 [4, 192, 256], P(None, 'lon')
Inputs may be any that keep to these rules, and one draw needn't show every extreme that they name: `obs_index`: index of a cell within the band's own block: level, then longitude within the band, then latitude. Each band uses its first obs_count slots; some band uses all 2048.
All inputs are finite; a program needn't handle non-finite values.
Results may differ from a plain program's by a relative error of at most 0.0001.
Values sent between devices are 32-bit elements; how exact they have to be, the bound alone decides.
A program may use at most 128 MiB of HBM per device.

v0:
```python
import jax
import jax.numpy as jnp
from jax import lax
from jax.sharding import PartitionSpec as P

KV = 2
KH = 4
ADV_STEPS = 2


def padded(block, sides, width):
    for axis, dim in sides:
        count = lax.axis_size(axis)
        forward = [(i, i + 1) for i in range(count - 1)]
        forward.append((count - 1, 0))
        backward = [(target, source) for source, target in forward]
        low = lax.ppermute(
            lax.slice_in_dim(block, block.shape[dim] - width, None, axis=dim), axis, forward
        )
        high = lax.ppermute(lax.slice_in_dim(block, 0, width, axis=dim), axis, backward)
        block = jnp.concatenate([low, block, high], axis=dim)
    return block


def update(centre, western, eastern, flow_lon, flow_lat):
    zero_col = jnp.zeros_like(centre[..., :1])
    south_boundary = jnp.concatenate([zero_col, centre[..., :-1]], axis=-1)
    northern = jnp.concatenate([centre[..., 1:], zero_col], axis=-1)
    result = centre - jnp.maximum(flow_lon, 0.0) * (centre - western)
    result = result - jnp.minimum(flow_lon, 0.0) * (eastern - centre)
    result = result - jnp.maximum(flow_lat, 0.0) * (centre - south_boundary)
    result = result - jnp.minimum(flow_lat, 0.0) * (northern - centre)
    return result


def per_device(
    members,
    courant_lon,
    courant_lat,
    vert_modes,
    horiz_modes,
    obs_index,
    obs_count,
    obs_value,
    obs_var,
):
    mem_dev, layer_tally, band_width, lat_rows = members.shape
    sample_tally_overall = mem_dev * lax.axis_size("mem")
    rim_depth = ADV_STEPS
    stacked = jnp.concatenate(
        [members.reshape(mem_dev * layer_tally, band_width, lat_rows), courant_lon, courant_lat],
        axis=0,
    )
    extended = padded(stacked, (("lon", 1),), rim_depth)
    split_at = mem_dev * layer_tally
    prognostic_vector = extended[:split_at].reshape(
        mem_dev, layer_tally, band_width + 2 * rim_depth, lat_rows
    )
    flow_lon_ext = extended[split_at : split_at + layer_tally]
    meridional_wind_padded = extended[split_at + layer_tally :]
    for section in range(rim_depth):
        out_cols = band_width + 2 * (rim_depth - 1 - section)
        first_col = section + 1
        prognostic_vector = update(
            prognostic_vector[:, :, 1 : out_cols + 1],
            prognostic_vector[:, :, 0:out_cols],
            prognostic_vector[:, :, 2 : out_cols + 2],
            flow_lon_ext[:, first_col : first_col + out_cols],
            meridional_wind_padded[:, first_col : first_col + out_cols],
        )
    sample_centroid = lax.psum(jnp.sum(prognostic_vector, axis=0), "mem") / sample_tally_overall
    sample_departure = prognostic_vector - sample_centroid[None]
    norm_scale = (sample_tally_overall - 1) ** (-0.5)
    obs_slots = obs_index.shape[0]
    band_cells = band_width * lat_rows
    level_idx = obs_index // band_cells
    within = obs_index % band_cells
    anomaly_obs = jnp.take(sample_departure.reshape(mem_dev, -1), obs_index, axis=1)
    mean_obs = jnp.take(sample_centroid.reshape(-1), obs_index)
    vert_obs = jnp.take(vert_modes, level_idx, axis=1)
    horiz_obs = jnp.take(horiz_modes.reshape(KH, -1), within, axis=1)
    modes_obs = (vert_obs[:, None, :] * horiz_obs[None, :, :]).reshape(KV * KH, obs_slots)
    live_mask = (jnp.arange(obs_slots, dtype=jnp.int32) < obs_count[0]).astype(jnp.float32)
    obs_perts = (
        anomaly_obs[:, None, :] * modes_obs[None, :, :] * (live_mask * norm_scale)[None, None, :]
    )
    obs_perts = obs_perts.reshape(mem_dev * KV * KH, obs_slots)
    inv_var = live_mask / obs_var
    innovation = obs_value - mean_obs
    all_perts = lax.all_gather(obs_perts, "mem", axis=0, tiled=True)
    gram_part = jnp.dot(all_perts * inv_var[None, :], all_perts.T, precision=lax.Precision.HIGHEST)
    side_part = jnp.dot(all_perts, inv_var * innovation, precision=lax.Precision.HIGHEST)
    gram_matrix, right_side = lax.psum((gram_part, side_part), "lon")
    system = jnp.eye(gram_matrix.shape[0], dtype=jnp.float32) + gram_matrix
    factor = jnp.linalg.cholesky(system)
    weights = jax.scipy.linalg.cho_solve((factor, True), right_side)
    w_mat = weights.reshape(sample_tally_overall, KV * KH)
    w_local = lax.dynamic_slice_in_dim(w_mat, lax.axis_index("mem") * mem_dev, mem_dev, 0)
    mode_coef = jnp.einsum(
        "mk,mlij->klij", w_local, sample_departure, precision=lax.Precision.HIGHEST
    )
    mode_coef = mode_coef.reshape(KV, KH, layer_tally, band_width, lat_rows)
    inc_part = (
        jnp.einsum(
            "al,bij,ablij->lij", vert_modes, horiz_modes, mode_coef, precision=lax.Precision.HIGHEST
        )
        * norm_scale
    )
    posterior_adjustment = lax.psum(inc_part, "mem")
    return (prognostic_vector, sample_centroid + posterior_adjustment)


def solution(mesh):
    placed = (
        P("mem", None, "lon", None),
        P(None, "lon", None),
        P(None, "lon", None),
        P(),
        P(None, "lon", None),
        P("lon"),
        P("lon"),
        P("lon"),
        P("lon"),
    )
    return jax.shard_map(
        per_device,
        mesh=mesh,
        in_specs=placed,
        out_specs=(P("mem", None, "lon", None), P(None, "lon", None)),
        check_vma=False,
    )
```

profile of v0, /device:TPU:0, one launch (start us, length us, event | category | flops | bytes accessed | tf_op | source)
XLA Modules:
  0.0 332.7 jit_solution(16638624239704680310)
XLA Ops:
  7.2 1.2 pad_maximum_fusion.5
  8.9 4.1 %collective-permute-start.1 = (f32[40,2,256]{2,1,0:T(2,128)S(1)}, f32[40,2,256]{2,1,0:T(2,128)S(1)}, u32[]{:S(2)}, u32[]{:S(2)}) collective-permute-start(f32[40,2,256]{2,1,0:T(2,128)S(1)} %get-tuple-element.36), channel_id=1, source_target_pairs={{4,0},{8,4},{12,8},{16,12},{20,16},{24,20},{28,24},{0,28},{5,1},{9... | collective-permute-start | bytes 245768 | tf_op jit(solution)/shard_map/ppermute | solution.py:20
  13.8 0.7 fusion.30
  14.5 0.8 copy.32
  15.2 5.5 %gather_fusion.1 = f32[2048,2]{1,0:T(8,128)S(1)} fusion(f32[2,4]{0,1:T(4,128)S(1)} %copy.32, s32[2048]{0:T(1024)S(1)} %get-tuple-element.46), kind=kCustom, calls=%fused_computation.1 | custom fusion | bytes 40960 | tf_op jit(solution)/shard_map/jit(_take)/gather | solution.py:80
  21.4 2.3 copy.34
  23.6 7.4 %gather_fusion.2 = f32[2048,4]{1,0:T(8,128)S(1)} fusion(f32[4,6144]{0,1:T(8,128)} %bitcast.119, s32[2048]{0:T(1024)S(1)} %get-tuple-element.47), kind=kCustom, calls=%fused_computation.2 | custom fusion | bytes 73728 | tf_op jit(solution)/shard_map/jit(_take)/gather | solution.py:81
  34.4 1.2 fusion.39
  35.6 41.8 %all-reduce.9.cloned.1.call-done = f32[4,24,256]{2,1,0:T(8,128)} async-done(((f32[4,24,256]{2,1,0:T(8,128)}), f32[4,24,256]{2,1,0:T(8,128)}) %all-reduce.9.cloned.1.call-update) | async-done | bytes 98320 | tf_op jit(solution)/shard_map/psum | solution.py:71
  77.5 0.9 broadcast_multiply_fusion
  78.5 6.6 %copy.30 = f32[8,4,24,256]{0,3,2,1:T(8,128)} copy(f32[8,4,24,256]{3,2,1,0:T(8,128)S(1)} %broadcast_subtract_fusion) | data formatting | bytes 1572864 | tf_op jit(solution)/shard_map/sub | solution.py:72
  85.1 11.8 %gather_fusion.3 = f32[2048]{0:T(1024)S(1)} fusion(f32[24576]{0:T(1024)S(1)} %bitcast.112, s32[2048]{0:T(1024)S(1)} %get-tuple-element.45), kind=kCustom, calls=%fused_computation.3 | custom fusion | bytes 24576 | tf_op jit(solution)/shard_map/jit(_take)/gather | solution.py:79
  96.9 10.0 %gather_fusion = f32[2048,8]{1,0:T(8,128)S(1)} fusion(f32[8,24576]{0,1:T(8,128)} %bitcast.113, s32[2048]{0:T(1024)S(1)} %get-tuple-element.45), kind=kCustom, calls=%fused_computation | custom fusion | bytes 139264 | tf_op jit(solution)/shard_map/jit(_take)/gather | solution.py:78
  107.6 0.9 bitcast_multiply_fusion
  108.8 35.2 %all-gather.2.cloned.1.call-done = f32[256,2048]{1,0:T(8,128)} async-done(((f32[64,2048]{1,0:T(8,128)}), f32[256,2048]{1,0:T(8,128)}) %all-gather.2.cloned.1.call-update) | async-done | bytes 2097168 | tf_op jit(solution)/shard_map/all_gather | solution.py:90
  144.0 5.0 %fusion = f32[256,256]{0,1:T(8,128)} fusion(f32[256,2048]{1,0:T(8,128)} %all-gather.2.cloned.1.call-done, f32[2048]{0:T(1024)S(1)} %get-tuple-element.19), kind=kOutput, calls=%fused_computation.6 | convolution fusion | flops 1611137024 | bytes 2367488 | tf_op jit(solution)/shard_map/dot_general | solution.py:91
  149.1 1.7 fusion.44
  150.8 16.6 %psum.30 = f32[256]{0:T(256)S(1)} all-reduce(f32[256]{0:T(256)S(1)} %bitcast.124), channel_id=1, replica_groups=mesh['lon'=8,'mem'=4] {'lon'}, use_global_device_ids=true, to_apply=%region_7.8 | all-reduce | flops 256 | bytes 2048 | tf_op jit(solution)/shard_map/psum | solution.py:93
  167.4 36.7 %all-reduce.11.cloned.1.call-done = f32[256,256]{0,1:T(8,128)} async-done(((f32[256,256]{0,1:T(8,128)}), f32[256,256]{0,1:T(8,128)}) %all-reduce.11.cloned.1.call-update) | async-done | bytes 262160 | tf_op jit(solution)/shard_map/psum | solution.py:93
  204.1 1.0 convert_add_fusion
  205.2 1.0 fusion.19
  206.2 11.7 %cholesky.50 = f32[128,128]{1,0:T(8,128)S(1)} custom-call(f32[128,128]{1,0:T(8,128)S(1)} %cholesky.118), custom_call_target="Cholesky" | custom-call | tf_op jit(solution)/shard_map/jit(cholesky)/cholesky | solution.py:95
  218.7 9.8 %custom-call.18 = f32[1,128,128]{1,2,0:T(8,128)S(1)} custom-call(f32[1,128,128]{2,1,0:T(8,128)S(1)} %get-tuple-element.44), custom_call_target="InvertDiagBlocksLowerTriangular" | custom-call | tf_op jit(solution)/shard_map/jit(cholesky)/cholesky | solution.py:95
  229.0 11.7 %cholesky.105 = f32[128,128]{1,0:T(8,128)S(1)} custom-call(f32[128,128]{1,0:T(8,128)S(1)} %convolution_subtract_fusion), custom_call_target="Cholesky" | custom-call | tf_op jit(solution)/shard_map/jit(cholesky)/cholesky | solution.py:95
  242.6 3.8 %while.1 = (s32[]{:T(128)}, f32[256,256]{1,0:T(8,128)S(1)}, s32[2,2]{1,0:T(2,128)S(1)}, f32[2,128,128]{2,1,0:T(8,128)S(1)}, s32[]{:T(128)}) while((s32[]{:T(128)}, f32[256,256]{1,0:T(8,128)S(1)}, s32[2,2]{1,0:T(2,128)S(1)}, f32[2,128,128]{2,1,0:T(8,128)S(1)}, s32[]{:T(128)}) %tuple.44), condition=%wide.while_cond, body=%wide.while_body.sunk | while | flops 2 | bytes 131189 | solution.py:96
  243.2 1.3 bitcast_dynamic-update-slice_fusion.2
  245.2 1.3 bitcast_dynamic-update-slice_fusion.2
  246.4 19.9 %custom-call.19 = f32[2,128,128]{1,2,0:T(8,128)S(1)} custom-call(f32[2,128,128]{2,1,0:T(8,128)S(1)} %get-tuple-element.9), custom_call_target="InvertDiagBlocksLowerTriangular" | custom-call | tf_op jit(solution)/shard_map/jit(_cho_solve)/triangular_solve | solution.py:96
  267.6 13.6 %fusion.31 = f32[8,4,24,256]{3,0,2,1:T(8,128)S(1)} fusion(f32[8,4,24,256]{0,3,2,1:T(8,128)} %copy.30, f32[32,8]{1,0:T(8,128)S(1)} %reshape.169, s32[]{:T(128)S(6)} %select_n.71), kind=kOutput, calls=%fused_computation.98 | convolution fusion | flops 18874368 | bytes 1576964 | tf_op jit(solution)/shard_map/mk,mlij->klij/dot_general | solution.py:99
  282.1 0.8 fusion.20
  283.6 41.0 %all-reduce.13.cloned.1.call-done = f32[4,24,256]{2,1,0:T(8,128)} async-done(((f32[4,24,256]{2,1,0:T(8,128)}), f32[4,24,256]{2,1,0:T(8,128)}) %all-reduce.13.cloned.1.call-update) | async-done | bytes 98320 | tf_op jit(solution)/shard_map/psum | solution.py:109
  324.6 1.5 fusion.38
  (85 shorter events, 11.7 us)
Async XLA Ops:
  7.2 70.3 %all-reduce.9.cloned.1.call-start = ((), (), s32[]{:S(2)}) async-start(), calls=%async_computation | async-start | bytes 196608 | tf_op jit(solution)/shard_map/psum | solution.py:71
  7.2 14.2 %copy-start.5 = (f32[4,24,256]{2,1,0:T(8,128)S(1)}, f32[4,24,256]{2,1,0:T(8,128)}, u32[]{:S(2)}) copy-start(f32[4,24,256]{2,1,0:T(8,128)} %param.13) | copy-start | bytes 294916
  8.4 24.1 %collective-permute-start = (f32[40,2,256]{2,1,0:T(2,128)S(1)}, f32[40,2,256]{2,1,0:T(2,128)S(1)}, u32[]{:S(2)}, u32[]{:S(2)}) collective-permute-start(f32[40,2,256]{2,1,0:T(2,128)S(1)} %get-tuple-element.35), channel_id=1, source_target_pairs={{0,4},{4,8},{8,12},{12,16},{16,20},{20,24},{24,28},{28,0},{1,5},{5... | collective-permute-start | bytes 245768 | tf_op jit(solution)/shard_map/ppermute | solution.py:17
  8.9 23.6 %collective-permute-start.1 = (f32[40,2,256]{2,1,0:T(2,128)S(1)}, f32[40,2,256]{2,1,0:T(2,128)S(1)}, u32[]{:S(2)}, u32[]{:S(2)}) collective-permute-start(f32[40,2,256]{2,1,0:T(2,128)S(1)} %get-tuple-element.36), channel_id=1, source_target_pairs={{4,0},{8,4},{12,8},{16,12},{20,16},{24,20},{28,24},{0,28},{5,1},{9... | collective-permute-start | bytes 245768 | tf_op jit(solution)/shard_map/ppermute | solution.py:20
  23.6 8.2 %copy-start.3 = (f32[4,24,256]{2,1,0:T(8,128)S(1)}, f32[4,24,256]{2,1,0:T(8,128)}, u32[]{:S(2)}) copy-start(f32[4,24,256]{2,1,0:T(8,128)} %param.11) | copy-start | bytes 294916
  23.6 8.2 %copy-start.4 = (f32[4,24,256]{2,1,0:T(8,128)S(1)}, f32[4,24,256]{2,1,0:T(8,128)}, u32[]{:S(2)}) copy-start(f32[4,24,256]{2,1,0:T(8,128)} %param.10) | copy-start | bytes 294916
  23.6 8.9 %copy-start.1 = (f32[8,4,24,256]{3,2,1,0:T(8,128)S(1)}, f32[8,4,24,256]{3,2,1,0:T(8,128)}, u32[]{:S(2)}) copy-start(f32[8,4,24,256]{3,2,1,0:T(8,128)} %param.9) | copy-start | bytes 2359300
  35.6 49.5 %copy-start.2 = (f32[8,4,24,256]{3,2,1,0:T(8,128)}, f32[8,4,24,256]{3,2,1,0:T(8,128)S(1)}, u32[]{:S(2)}) copy-start(f32[8,4,24,256]{3,2,1,0:T(8,128)S(1)} %get-tuple-element.22) | copy-start | bytes 2359300
  35.6 108.4 %all-gather.2.cloned.1.call-start = ((), (), s32[]{:S(2)}) async-start(), calls=%async_computation.1 | async-start | bytes 2621440 | tf_op jit(solution)/shard_map/all_gather | solution.py:90
  85.1 21.9 %copy-start.7 = (s32[2048]{0:T(1024)S(1)}, s32[2048]{0:T(1024)}, u32[]{:S(2)}) copy-start(s32[2048]{0:T(1024)} %param.14) | copy-start | bytes 24580
  85.1 21.9 %copy-start.8 = (f32[2048]{0:T(1024)S(1)}, f32[2048]{0:T(1024)}, u32[]{:S(2)}) copy-start(f32[2048]{0:T(1024)} %param.16) | copy-start | bytes 24580
  85.1 21.9 %copy-start.9 = (f32[2048]{0:T(1024)S(1)}, f32[2048]{0:T(1024)}, u32[]{:S(2)}) copy-start(f32[2048]{0:T(1024)} %param.17) | copy-start | bytes 24580
  107.0 1.6 copy-start.10
  108.5 95.6 %all-reduce.11.cloned.1.call-start = ((), (), s32[]{:S(2)}) async-start(), calls=%async_computation.2 | async-start | bytes 524288 | tf_op jit(solution)/shard_map/psum | solution.py:93
  144.0 5.1 %copy-start = (f32[256,2048]{1,0:T(8,128)S(1)}, f32[256,2048]{1,0:T(8,128)}, u32[]{:S(2)}) copy-start(f32[256,2048]{1,0:T(8,128)} %all-gather.2.cloned.1.call-done) | copy-start | bytes 6291460
  149.0 175.6 %all-reduce.13.cloned.1.call-start = ((), (), s32[]{:S(2)}) async-start(), calls=%async_computation.3 | async-start | bytes 196608 | tf_op jit(solution)/shard_map/psum | solution.py:109
  281.2 43.4 %copy-start.6 = (f32[4,24,256]{2,1,0:T(8,128)S(1)}, f32[4,24,256]{2,1,0:T(8,128)}, u32[]{:S(2)}) copy-start(f32[4,24,256]{2,1,0:T(8,128)} %all-reduce.9.cloned.1.call-done) | copy-start | bytes 294916
Sparse Core Ops, SparseCore 0:
  35.7 41.7 all-reduce.8
  108.7 35.2 all-gather.1
  149.1 54.9 all-reduce.10
  283.8 40.8 all-reduce.12
where the time goes:
time: 333 us
  waiting for transfers between devices  155 us (47%)
  other arithmetic  67 us (20%)
  local copies, waits for them, and re-layouts  50.6 us (15%)
  matrix products  22.8 us (7%)
  blocking collectives  16.6 us (5%)
  between operations  16 us (5%)
  starting transfers between devices  4.77 us (1%)
    psum x1, waiting for transfers between devices, per_device(): lax.psum(jnp.sum(prognostic_vector, axis=0), 'mem') / sample_tally_overall  41.8 us
    psum x1, waiting for transfers between devices, per_device(): posterior_adjustment = lax.psum(inc_part, 'mem')  41 us
    psum x1, waiting for transfers between devices, per_device(): gram_matrix, right_side = lax.psum((gram_part, side_part), 'lon')  36.7 us
    all_gather x1, waiting for transfers between devices, per_device(): all_perts = lax.all_gather(obs_perts, 'mem', axis=0, tiled=True)  35.2 us
    another operation x7, other arithmetic, per_device(): factor = jnp.linalg.cholesky(system)  34.6 us
    another operation x4, other arithmetic, per_device(): weights = jax.scipy.linalg.cho_solve((factor, True), right_side)  20 us
    psum x1, blocking collectives, per_device(): gram_matrix, right_side = lax.psum((gram_part, side_part), 'lon')  16.6 us
    dot_general x1, matrix products, per_device(): jnp.einsum('mk,mlij->klij', w_local, sample_departure, precision=lax.Prec...  13.6 us
  transfers between devices with their start and end apart: 6, of which 4 were waited for; matrix products, arithmetic and copies ran while one was open for 6% of the time, Pallas kernels for 0%

commit v1 on v0

--- a/solution.py
+++ b/solution.py
@@ -87,7 +87,14 @@
     obs_perts = obs_perts.reshape(mem_dev * KV * KH, obs_slots)
     inv_var = live_mask / obs_var
     innovation = obs_value - mean_obs
-    all_perts = lax.all_gather(obs_perts, "mem", axis=0, tiled=True)
+    count_2 = lax.axis_size("mem")
+    forward_2 = [(i_2, (i_2 + 1) % count_2) for i_2 in range(count_2)]
+    parts = [obs_perts]
+    for far in range(1, count_2):
+        parts = [lax.ppermute(parts[0], "mem", forward_2), *parts]
+    result_2 = jnp.concatenate(parts, axis=0)
+    shift = (lax.axis_index("mem") + 1) * parts[-1].shape[0]
+    all_perts = jnp.roll(result_2, shift, axis=0)
     gram_part = jnp.dot(all_perts * inv_var[None, :], all_perts.T, precision=lax.Precision.HIGHEST)
     side_part = jnp.dot(all_perts, inv_var * innovation, precision=lax.Precision.HIGHEST)
     gram_matrix, right_side = lax.psum((gram_part, side_part), "lon")

time: 333 us -> 337 us (1.012)
    ppermute x0 -> x3, waiting for transfers between devices: none -> 37.6 us  [per_device(): parts = [lax.ppermute(parts[0], 'mem', forward_2), *parts]]
    all_gather x1 -> x0, waiting for transfers between devices: 35.2 us -> none  [per_device(): all_perts = lax.all_gather(obs_perts, 'mem', axis=0, tiled=True)]
  transfers between devices with their start and end apart: 6 -> 8, of which waited for: 4 -> 6; matrix products, arithmetic and copies ran while one was open for 6% -> 7% of each run, Pallas kernels for 0% -> 0%
where the time goes in v1:
time: 337 us; the launch traced here: 336 us
  waiting for transfers between devices  158 us (47%)
  other arithmetic  66.3 us (20%)
  local copies, waits for them, and re-layouts  52.9 us (16%)
  matrix products  22.1 us (7%)
  between operations  16 us (5%)
  blocking collectives  13.9 us (4%)
  starting transfers between devices  6.77 us (2%)
    psum x1, waiting for transfers between devices, per_device(): lax.psum(jnp.sum(prognostic_vector, axis=0), 'mem') / sample_tally_overall  41.8 us
    psum x1, waiting for transfers between devices, per_device(): posterior_adjustment = lax.psum(inc_part, 'mem')  41 us
    psum x1, waiting for transfers between devices, per_device(): gram_matrix, right_side = lax.psum((gram_part, side_part), 'lon')  37.7 us
    ppermute x3, waiting for transfers between devices, per_device(): parts = [lax.ppermute(parts[0], 'mem', forward_2), *parts]  37.6 us
    another operation x7, other arithmetic, per_device(): factor = jnp.linalg.cholesky(system)  34.6 us
    another operation x4, other arithmetic, per_device(): weights = jax.scipy.linalg.cho_solve((factor, True), right_side)  20 us
    psum x1, blocking collectives, per_device(): gram_matrix, right_side = lax.psum((gram_part, side_part), 'lon')  13.9 us
    dot_general x1, matrix products, per_device(): jnp.einsum('mk,mlij->klij', w_local, sample_departure, precision=lax.Prec...  13.6 us
  transfers between devices with their start and end apart: 8, of which 6 were waited for; matrix products, arithmetic and copies ran while one was open for 7% of the time, Pallas kernels for 0%

profile of v1, /device:TPU:0, one launch (start us, length us, event | category | flops | bytes accessed | tf_op | source)
XLA Modules:
  0.0 336.1 jit_solution(8426013771274765417)
XLA Ops:
  7.2 1.2 pad_maximum_fusion.5
  8.9 4.1 %collective-permute-start.1 = (f32[40,2,256]{2,1,0:T(2,128)S(1)}, f32[40,2,256]{2,1,0:T(2,128)S(1)}, u32[]{:S(2)}, u32[]{:S(2)}) collective-permute-start(f32[40,2,256]{2,1,0:T(2,128)S(1)} %get-tuple-element.36), channel_id=1, source_target_pairs={{4,0},{8,4},{12,8},{16,12},{20,16},{24,20},{28,24},{0,28},{5,1},{9... | collective-permute-start | bytes 245768 | tf_op jit(solution)/shard_map/ppermute | solution.py:20
  14.4 3.0 copy.34
  17.5 7.4 %gather_fusion.2 = f32[2048,4]{1,0:T(8,128)S(1)} fusion(f32[4,6144]{0,1:T(8,128)} %bitcast.121, s32[2048]{0:T(1024)S(1)} %get-tuple-element.47), kind=kCustom, calls=%fused_computation.2 | custom fusion | bytes 73728 | tf_op jit(solution)/shard_map/jit(_take)/gather | solution.py:81
  25.7 5.5 %gather_fusion.1 = f32[2048,2]{1,0:T(8,128)S(1)} fusion(f32[2,4]{0,1:T(4,128)S(1)} %copy.32, s32[2048]{0:T(1024)S(1)} %get-tuple-element.46), kind=kCustom, calls=%fused_computation.1 | custom fusion | bytes 40960 | tf_op jit(solution)/shard_map/jit(_take)/gather | solution.py:80
  34.5 1.2 fusion.46
  35.7 41.8 %all-reduce.9.cloned.1.call-done = f32[4,24,256]{2,1,0:T(8,128)} async-done(((f32[4,24,256]{2,1,0:T(8,128)}), f32[4,24,256]{2,1,0:T(8,128)}) %all-reduce.9.cloned.1.call-update) | async-done | bytes 98320 | tf_op jit(solution)/shard_map/psum | solution.py:71
  77.6 0.9 broadcast_multiply_fusion
  78.5 6.6 %copy.30 = f32[8,4,24,256]{0,3,2,1:T(8,128)} copy(f32[8,4,24,256]{3,2,1,0:T(8,128)S(1)} %broadcast_subtract_fusion) | data formatting | bytes 1572864 | tf_op jit(solution)/shard_map/sub | solution.py:72
  85.2 10.0 %gather_fusion = f32[2048,8]{1,0:T(8,128)S(1)} fusion(f32[8,24576]{0,1:T(8,128)} %bitcast.115, s32[2048]{0:T(1024)S(1)} %get-tuple-element.45), kind=kCustom, calls=%fused_computation | custom fusion | bytes 139264 | tf_op jit(solution)/shard_map/jit(_take)/gather | solution.py:78
  95.3 11.8 %gather_fusion.3 = f32[2048]{0:T(1024)S(1)} fusion(f32[24576]{0:T(1024)S(1)} %bitcast.114, s32[2048]{0:T(1024)S(1)} %get-tuple-element.45), kind=kCustom, calls=%fused_computation.3 | custom fusion | bytes 24576 | tf_op jit(solution)/shard_map/jit(_take)/gather | solution.py:79
  107.8 1.5 collective-permute-start.2
  109.3 12.7 %collective-permute-done.2 = f32[64,2048]{1,0:T(8,128)S(1)} collective-permute-done((f32[64,2048]{1,0:T(8,128)S(1)}, f32[64,2048]{1,0:T(8,128)S(1)}, u32[]{:S(2)}, u32[]{:S(2)}) %collective-permute-start.2) | collective-permute-done | bytes 524320 | tf_op jit(solution)/shard_map/ppermute | solution.py:94
  122.5 12.7 %collective-permute-done.3 = f32[64,2048]{1,0:T(8,128)S(1)} collective-permute-done((f32[64,2048]{1,0:T(8,128)S(1)}, f32[64,2048]{1,0:T(8,128)S(1)}, u32[]{:S(2)}, u32[]{:S(2)}) %collective-permute-start.3) | collective-permute-done | bytes 524320 | tf_op jit(solution)/shard_map/ppermute | solution.py:94
  135.4 12.2 %collective-permute-done.4 = f32[64,2048]{1,0:T(8,128)S(1)} collective-permute-done((f32[64,2048]{1,0:T(8,128)S(1)}, f32[64,2048]{1,0:T(8,128)S(1)}, u32[]{:S(2)}, u32[]{:S(2)}) %collective-permute-start.4) | collective-permute-done | bytes 524320 | tf_op jit(solution)/shard_map/ppermute | solution.py:94
  148.0 1.9 copy-done
  149.9 2.7 fusion
  152.6 3.3 fusion.3
  155.9 13.9 %psum.30 = f32[256]{0:T(256)S(1)} all-reduce(f32[256]{0:T(256)S(1)} %bitcast.126), channel_id=1, replica_groups=mesh['lon'=8,'mem'=4] {'lon'}, use_global_device_ids=true, to_apply=%region_7.8 | all-reduce | flops 256 | bytes 2048 | tf_op jit(solution)/shard_map/psum | solution.py:100
  169.8 37.7 %all-reduce.11.cloned.1.call-done = f32[256,256]{0,1:T(8,128)} async-done(((f32[256,256]{0,1:T(8,128)}), f32[256,256]{0,1:T(8,128)}) %all-reduce.11.cloned.1.call-update) | async-done | bytes 262160 | tf_op jit(solution)/shard_map/psum | solution.py:100
  207.5 1.0 convert_add_fusion
  208.6 1.0 fusion.24
  209.6 11.7 %cholesky.50 = f32[128,128]{1,0:T(8,128)S(1)} custom-call(f32[128,128]{1,0:T(8,128)S(1)} %cholesky.118), custom_call_target="Cholesky" | custom-call | tf_op jit(solution)/shard_map/jit(cholesky)/cholesky | solution.py:102
  221.4 9.8 %custom-call.18 = f32[1,128,128]{1,2,0:T(8,128)S(1)} custom-call(f32[1,128,128]{2,1,0:T(8,128)S(1)} %get-tuple-element.44), custom_call_target="InvertDiagBlocksLowerTriangular" | custom-call | tf_op jit(solution)/shard_map/jit(cholesky)/cholesky | solution.py:102
  231.7 11.7 %cholesky.105 = f32[128,128]{1,0:T(8,128)S(1)} custom-call(f32[128,128]{1,0:T(8,128)S(1)} %convolution_subtract_fusion), custom_call_target="Cholesky" | custom-call | tf_op jit(solution)/shard_map/jit(cholesky)/cholesky | solution.py:102
  246.0 3.8 %while.1 = (s32[]{:T(128)}, f32[256,256]{1,0:T(8,128)S(1)}, s32[2,2]{1,0:T(2,128)S(1)}, f32[2,128,128]{2,1,0:T(8,128)S(1)}, s32[]{:T(128)}) while((s32[]{:T(128)}, f32[256,256]{1,0:T(8,128)S(1)}, s32[2,2]{1,0:T(2,128)S(1)}, f32[2,128,128]{2,1,0:T(8,128)S(1)}, s32[]{:T(128)}) %tuple.44), condition=%wide.while_cond, body=%wide.while_body.sunk | while | flops 2 | bytes 131181 | solution.py:103
  246.6 1.3 bitcast_dynamic-update-slice_fusion.2
  248.5 1.3 bitcast_dynamic-update-slice_fusion.2
  249.8 19.9 %custom-call.19 = f32[2,128,128]{1,2,0:T(8,128)S(1)} custom-call(f32[2,128,128]{2,1,0:T(8,128)S(1)} %get-tuple-element.9), custom_call_target="InvertDiagBlocksLowerTriangular" | custom-call | tf_op jit(solution)/shard_map/jit(_cho_solve)/triangular_solve | solution.py:103
  271.0 13.6 %fusion.36 = f32[8,4,24,256]{3,0,2,1:T(8,128)S(1)} fusion(f32[8,4,24,256]{0,3,2,1:T(8,128)} %copy.30, f32[32,8]{1,0:T(8,128)S(1)} %reshape.169, s32[]{:T(128)S(6)} %select_n.85), kind=kOutput, calls=%fused_computation.109 | convolution fusion | flops 18874368 | bytes 1576964 | tf_op jit(solution)/shard_map/mk,mlij->klij/dot_general | solution.py:106
  287.0 41.0 %all-reduce.13.cloned.1.call-done = f32[4,24,256]{2,1,0:T(8,128)} async-done(((f32[4,24,256]{2,1,0:T(8,128)}), f32[4,24,256]{2,1,0:T(8,128)}) %all-reduce.13.cloned.1.call-update) | async-done | bytes 98320 | tf_op jit(solution)/shard_map/psum | solution.py:116
  328.0 1.5 fusion.45
  (96 shorter events, 14.2 us)
Async XLA Ops:
  7.2 18.4 %copy-start.10 = (f32[2,4]{1,0:T(2,128)S(1)}, f32[2,4]{1,0:T(2,128)}, u32[]{:S(2)}) copy-start(f32[2,4]{1,0:T(2,128)} %param.12) | copy-start | bytes 100
  7.2 70.4 %all-reduce.9.cloned.1.call-start = ((), (), s32[]{:S(2)}) async-start(), calls=%async_computation | async-start | bytes 196608 | tf_op jit(solution)/shard_map/psum | solution.py:71
  8.4 24.2 %collective-permute-start = (f32[40,2,256]{2,1,0:T(2,128)S(1)}, f32[40,2,256]{2,1,0:T(2,128)S(1)}, u32[]{:S(2)}, u32[]{:S(2)}) collective-permute-start(f32[40,2,256]{2,1,0:T(2,128)S(1)} %get-tuple-element.35), channel_id=1, source_target_pairs={{0,4},{4,8},{8,12},{12,16},{16,20},{20,24},{24,28},{28,0},{1,5},{5... | collective-permute-start | bytes 245768 | tf_op jit(solution)/shard_map/ppermute | solution.py:17
  8.9 23.7 %collective-permute-start.1 = (f32[40,2,256]{2,1,0:T(2,128)S(1)}, f32[40,2,256]{2,1,0:T(2,128)S(1)}, u32[]{:S(2)}, u32[]{:S(2)}) collective-permute-start(f32[40,2,256]{2,1,0:T(2,128)S(1)} %get-tuple-element.36), channel_id=1, source_target_pairs={{4,0},{8,4},{12,8},{16,12},{20,16},{24,20},{28,24},{0,28},{5,1},{9... | collective-permute-start | bytes 245768 | tf_op jit(solution)/shard_map/ppermute | solution.py:20
  17.5 14.4 %copy-start.3 = (f32[4,24,256]{2,1,0:T(8,128)S(1)}, f32[4,24,256]{2,1,0:T(8,128)}, u32[]{:S(2)}) copy-start(f32[4,24,256]{2,1,0:T(8,128)} %param.11) | copy-start | bytes 294916
  17.5 14.4 %copy-start.4 = (f32[4,24,256]{2,1,0:T(8,128)S(1)}, f32[4,24,256]{2,1,0:T(8,128)}, u32[]{:S(2)}) copy-start(f32[4,24,256]{2,1,0:T(8,128)} %param.10) | copy-start | bytes 294916
  17.5 15.2 %copy-start.1 = (f32[8,4,24,256]{3,2,1,0:T(8,128)S(1)}, f32[8,4,24,256]{3,2,1,0:T(8,128)}, u32[]{:S(2)}) copy-start(f32[8,4,24,256]{3,2,1,0:T(8,128)} %param.9) | copy-start | bytes 2359300
  35.6 49.5 %copy-start.2 = (f32[8,4,24,256]{3,2,1,0:T(8,128)}, f32[8,4,24,256]{3,2,1,0:T(8,128)S(1)}, u32[]{:S(2)}) copy-start(f32[8,4,24,256]{3,2,1,0:T(8,128)S(1)} %get-tuple-element.22) | copy-start | bytes 2359300
  35.7 171.8 %all-reduce.11.cloned.1.call-start = ((), (), s32[]{:S(2)}) async-start(), calls=%async_computation.1 | async-start | bytes 524288 | tf_op jit(solution)/shard_map/psum | solution.py:100
  95.2 11.8 %copy-start.7 = (s32[2048]{0:T(1024)S(1)}, s32[2048]{0:T(1024)}, u32[]{:S(2)}) copy-start(s32[2048]{0:T(1024)} %param.14) | copy-start | bytes 24580
  95.2 11.8 %copy-start.8 = (f32[2048]{0:T(1024)S(1)}, f32[2048]{0:T(1024)}, u32[]{:S(2)}) copy-start(f32[2048]{0:T(1024)} %param.16) | copy-start | bytes 24580
  95.2 11.8 %copy-start.9 = (f32[2048]{0:T(1024)S(1)}, f32[2048]{0:T(1024)}, u32[]{:S(2)}) copy-start(f32[2048]{0:T(1024)} %param.17) | copy-start | bytes 24580
  95.2 40.0 %copy-start.5 = (f32[4,24,256]{2,1,0:T(8,128)S(1)}, f32[4,24,256]{2,1,0:T(8,128)}, u32[]{:S(2)}) copy-start(f32[4,24,256]{2,1,0:T(8,128)} %param.13) | copy-start | bytes 294916
  107.8 14.2 %collective-permute-start.2 = (f32[64,2048]{1,0:T(8,128)S(1)}, f32[64,2048]{1,0:T(8,128)S(1)}, u32[]{:S(2)}, u32[]{:S(2)}) collective-permute-start(f32[64,2048]{1,0:T(8,128)S(1)} %bitcast_multiply_fusion), channel_id=1, source_target_pairs={{0,1},{1,2},{2,3},{3,0},{4,5},{5,6},{6,7},{7,4},{8,9},{9,10},{10,1... | collective-permute-start | bytes 1572872 | tf_op jit(solution)/shard_map/ppermute | solution.py:94
  122.0 13.2 %collective-permute-start.3 = (f32[64,2048]{1,0:T(8,128)S(1)}, f32[64,2048]{1,0:T(8,128)S(1)}, u32[]{:S(2)}, u32[]{:S(2)}) collective-permute-start(f32[64,2048]{1,0:T(8,128)S(1)} %collective-permute-done.2), channel_id=1, source_target_pairs={{0,1},{1,2},{2,3},{3,0},{4,5},{5,6},{6,7},{7,4},{8,9},{9,10},{10,1... | collective-permute-start | bytes 1572872 | tf_op jit(solution)/shard_map/ppermute | solution.py:94
  135.3 12.3 %collective-permute-start.4 = (f32[64,2048]{1,0:T(8,128)S(1)}, f32[64,2048]{1,0:T(8,128)S(1)}, u32[]{:S(2)}, u32[]{:S(2)}) collective-permute-start(f32[64,2048]{1,0:T(8,128)S(1)} %collective-permute-done.3), channel_id=1, source_target_pairs={{0,1},{1,2},{2,3},{3,0},{4,5},{5,6},{6,7},{7,4},{8,9},{9,10},{10,1... | collective-permute-start | bytes 1572872 | tf_op jit(solution)/shard_map/ppermute | solution.py:94
  148.0 1.9 copy-start
  152.6 175.4 %all-reduce.13.cloned.1.call-start = ((), (), s32[]{:S(2)}) async-start(), calls=%async_computation.2 | async-start | bytes 196608 | tf_op jit(solution)/shard_map/psum | solution.py:116
  271.0 57.0 %copy-start.6 = (f32[4,24,256]{2,1,0:T(8,128)S(1)}, f32[4,24,256]{2,1,0:T(8,128)}, u32[]{:S(2)}) copy-start(f32[4,24,256]{2,1,0:T(8,128)} %all-reduce.9.cloned.1.call-done) | copy-start | bytes 294916
Sparse Core Ops, SparseCore 0:
  35.8 41.7 all-reduce.8
  152.7 54.7 all-reduce.10
  287.1 40.8 all-reduce.12
